TPU v7x, 32 devices: a whole 2x2x4 slice. The times are simulated.
32 devices in a mesh: slab: 2 (over x), blk: 16 (over z, y, core).
Axes of the slice: x: 2, y: 2, z: 4, core: 2. Of those that a mesh axis runs over, the one named last changes fastest.
Arguments:
- transmit: bfloat16 [2, 1024, 2048], P('slab', 'blk'), may hold values from -0.125 to 0.125
- reflect: bfloat16 [2, 2, 1024, 2048], P('slab', None, 'blk'), may hold values from -0.07910156 to 0.07910156
- source_amp: bfloat16 [512, 2048], P('blk'), may hold values from -6 to 6
- source_cell: int32 [512], P('blk'), may hold values from 0 to 1023
- source_slab: int32 [512], P('blk'), may hold values from 0 to 1
Outputs:
- sweep_out: float32 [2, 512, 2048], P('slab', 'blk')
All inputs are finite; a program needn't handle non-finite values.
Results may differ from a plain program's by a relative error of at most 0.018.
Values may be sent and summed in bfloat16 or wider, within the bound.
A program may use at most 64 MiB of HBM per device.

v0:
```python
import jax
import jax.numpy as jnp
from jax import lax
from jax.sharding import PartitionSpec as P


def shifted(block, axis, distance):
    devices = range(lax.axis_size(axis))
    route = [(i - distance, i) for i in devices if i - distance in devices]
    return lax.ppermute(block, axis, route)


def transposed(matrix):
    half_width = matrix.shape[0]
    return jnp.concatenate([matrix[:, :half_width].T, matrix[:, half_width:].T], 1)


def complex_rows(left_rows, right_matrix):
    inner_width = right_matrix.shape[0]
    outer_width = right_matrix.shape[1] // 2
    row_count = left_rows.shape[0]
    stacked = jnp.concatenate([left_rows[:, :inner_width], left_rows[:, inner_width:]], 0)
    product = jnp.dot(stacked, right_matrix, preferred_element_type=jnp.float32)
    real_out = product[:row_count, :outer_width] - product[row_count:, outer_width:]
    imag_out = product[:row_count, outer_width:] + product[row_count:, :outer_width]
    return jnp.concatenate([real_out, imag_out], 1)


def body(transmit, reflect, source_amp, source_cell, source_slab):
    trans_local = transmit[0]
    refl_local = reflect[0]
    half_width = source_amp.shape[1] // 2
    refl_second = lax.all_gather(refl_local[1], "blk", axis=0, tiled=True)
    coupling = complex_rows(refl_local[0], refl_second).astype(jnp.bfloat16)
    start_rows = trans_local.astype(jnp.float32)
    piece_rows = lax.all_gather(trans_local, "blk", axis=0, tiled=True)
    piece_count = piece_rows.shape[0]
    real_cols = lax.slice_in_dim(coupling, 0, piece_count, axis=1)
    imag_cols = lax.dynamic_slice_in_dim(coupling, half_width, piece_count, 1)
    left_rows = jnp.concatenate([real_cols, imag_cols], 1)
    joined = (start_rows + complex_rows(left_rows, piece_rows)).astype(jnp.bfloat16)
    slab_matrix = lax.all_gather(joined, "blk", axis=0, tiled=True)
    back_matrix = transposed(slab_matrix)
    cell_index = lax.iota(jnp.int32, half_width)
    offset = (cell_index[None, :] - source_cell[:, None]) % half_width
    inside = offset < half_width // 4
    here = source_slab == lax.axis_index("slab")
    keep = inside & here[:, None]
    keep = jnp.concatenate([keep, keep], 1)
    forcing = jnp.where(keep, source_amp, jnp.zeros_like(source_amp))
    chain_length = lax.axis_size("slab")
    carried = forcing
    for sweep_step in range(chain_length - 1):
        arrived = shifted(carried, "slab", 1)
        carried = (forcing.astype(jnp.float32) + complex_rows(arrived, slab_matrix)).astype(
            jnp.bfloat16
        )
    current = carried.astype(jnp.float32)
    for sweep_step in range(chain_length - 1):
        message = complex_rows(current.astype(jnp.bfloat16), back_matrix).astype(jnp.bfloat16)
        arrived = shifted(message, "slab", -1)
        current = carried.astype(jnp.float32) + arrived.astype(jnp.float32)
    return current[None]


def solution(mesh):
    return jax.shard_map(
        body,
        mesh=mesh,
        in_specs=(
            P("slab", "blk", None),
            P("slab", None, "blk", None),
            P("blk", None),
            P("blk"),
            P("blk"),
        ),
        out_specs=P("slab", "blk", None),
        check_vma=False,
    )
```

profile of v0, /device:TPU:0, one launch (start us, length us, event | category | flops | bytes accessed | tf_op | source)
XLA Modules:
  0.0 186.9 jit_solution(4141823036874665269)
XLA Ops:
  6.5 0.0 all-gather.8.cloned.1.call-start
  6.5 1.8 slice_bitcast_fusion.2
  8.3 0.0 all-gather.8.cloned.1.call-update
  8.3 0.0 all-gather.10.cloned.1.call-start
  8.4 0.7 all-gather.10.cloned.1.call-update
  9.1 0.0 all-gather.6.cloned.1.call-start
  9.2 53.5 %all-gather.8.cloned.1.call-done = bf16[1,1,1024,2048]{3,2,1,0:T(8,128)(2,1)} async-done(((bf16[1,1,64,2048]{3,2,1,0:T(8,128)(2,1)}), bf16[1,1,1024,2048]{3,2,1,0:T(8,128)(2,1)}) %all-gather.8.cloned.1.call-update) | async-done | bytes 4194320 | tf_op jit(solution)/shard_map/all_gather | solution.py:33
  62.6 2.9 %fusion.6 = f32[128,2048]{1,0:T(8,128)S(1)} fusion(bf16[1,1,1024,2048]{3,2,1,0:T(8,128)(2,1)} %all-gather.8.cloned.1.call-done, bf16[64,1024]{1,0:T(8,128)(2,1)S(1)} %get-tuple-element.18, bf16[64,1024]{1,0:T(8,128)(2,1)S(1)} %get-tuple-element.17), kind=kOutput, calls=%fused_computation.6 | convolution fusion | flops 537395200 | bytes 5505024 | tf_op jit(solution)/shard_map/dot_general | solution.py:23
  65.5 0.0 copy-start.1
  65.5 0.1 fusion.10
  65.6 48.1 %all-gather.10.cloned.1.call-done = bf16[1,1024,2048]{2,1,0:T(8,128)(2,1)} async-done(((bf16[1,64,2048]{2,1,0:T(8,128)(2,1)}), bf16[1,1024,2048]{2,1,0:T(8,128)(2,1)}) %all-gather.10.cloned.1.call-update) | async-done | bytes 4194320 | tf_op jit(solution)/shard_map/all_gather | solution.py:36
  113.7 0.0 copy-start.4
  113.7 0.0 copy-start.3
  113.7 0.0 copy-start.2
  113.7 2.9 %fusion.4 = f32[128,2048]{1,0:T(8,128)S(1)} fusion(bf16[1,1024,2048]{2,1,0:T(8,128)(2,1)} %all-gather.10.cloned.1.call-done, bf16[64,1024]{1,0:T(8,128)(2,1)S(1)} %get-tuple-element.10, bf16[64,1024]{1,0:T(8,128)(2,1)S(1)} %get-tuple-element.9), kind=kOutput, calls=%fused_computation.4 | convolution fusion | flops 537395200 | bytes 5505024 | tf_op jit(solution)/shard_map/dot_general | solution.py:23
  116.7 0.1 slice_subtract_fusion
  116.7 0.0 copy-done.1
  116.8 0.8 fusion.8
  117.5 0.0 all-gather.6.cloned.1.call-update
  117.6 0.0 copy-done.4
  117.6 0.0 copy-done.3
  117.6 0.1 fusion.32
  117.7 0.0 copy-done.2
  117.8 3.4 %collective-permute-start = (bf16[32,2048]{1,0:T(8,128)(2,1)S(1)}, bf16[32,2048]{1,0:T(8,128)(2,1)S(1)}, u32[]{:S(2)}, u32[]{:S(2)}) collective-permute-start(bf16[32,2048]{1,0:T(8,128)(2,1)S(1)} %add_select_fusion), channel_id=1, source_target_pairs={{0,16},{1,17},{2,18},{3,19},{4,20},{5,21},{6,22},{7,23},{8,24},{9,... | collective-permute-start | bytes 393224 | tf_op jit(solution)/shard_map/ppermute | solution.py:10
  121.2 3.1 %collective-permute-done = bf16[32,2048]{1,0:T(8,128)(2,1)S(1)} collective-permute-done((bf16[32,2048]{1,0:T(8,128)(2,1)S(1)}, bf16[32,2048]{1,0:T(8,128)(2,1)S(1)}, u32[]{:S(2)}, u32[]{:S(2)}) %collective-permute-start) | collective-permute-done | bytes 131104 | tf_op jit(solution)/shard_map/ppermute | solution.py:10
  124.3 42.3 %all-gather.6.cloned.1.call-done = bf16[1024,2048]{1,0:T(8,128)(2,1)} async-done(((bf16[64,2048]{1,0:T(8,128)(2,1)}), bf16[1024,2048]{1,0:T(8,128)(2,1)}) %all-gather.6.cloned.1.call-update) | async-done | bytes 4194320 | tf_op jit(solution)/shard_map/all_gather | solution.py:42
  166.6 0.0 copy-start
  166.6 3.2 %fusion.22 = f32[64,2048]{1,0:T(8,128)S(1)} fusion(bf16[1024,2048]{1,0:T(8,128)(2,1)} %all-gather.6.cloned.1.call-done, bf16[32,1024]{1,0:T(8,128)(2,1)S(1)} %get-tuple-element.22, bf16[32,1024]{1,0:T(8,128)(2,1)S(1)} %get-tuple-element.21), kind=kOutput, calls=%fused_computation.40 | convolution fusion | flops 268697600 | bytes 4849664 | tf_op jit(solution)/shard_map/dot_general | solution.py:23
  169.9 0.2 copy-done
  170.1 0.5 slice_bitcast_fusion.1
  170.6 1.4 fusion
  172.1 1.3 collective-permute-start.1
  173.4 6.2 %collective-permute-done.1 = bf16[32,2048]{1,0:T(8,128)(2,1)S(1)} collective-permute-done((bf16[32,2048]{1,0:T(8,128)(2,1)S(1)}, bf16[32,2048]{1,0:T(8,128)(2,1)S(1)}, u32[]{:S(2)}, u32[]{:S(2)}) %collective-permute-start.1) | collective-permute-done | bytes 131104 | tf_op jit(solution)/shard_map/ppermute | solution.py:10
  179.6 0.7 add_bitcast_fusion
  (9 shorter events, 0.2 us)
Async XLA Ops:
  6.5 56.1 %all-gather.8.cloned.1.call-start = ((), (), s32[]{:S(2)}) async-start(), calls=%async_computation.1 | async-start | bytes 4456448 | tf_op jit(solution)/shard_map/all_gather | solution.py:33
  8.3 105.4 %all-gather.10.cloned.1.call-start = ((), (), s32[]{:S(2)}) async-start(), calls=%async_computation.2 | async-start | bytes 4456448 | tf_op jit(solution)/shard_map/all_gather | solution.py:36
  9.1 157.5 %all-gather.6.cloned.1.call-start = ((), (), s32[]{:S(2)}) async-start(), calls=%async_computation | async-start | bytes 4456448 | tf_op jit(solution)/shard_map/all_gather | solution.py:42
  65.5 51.2 %copy-start.1 = (bf16[1,64,2048]{2,1,0:T(8,128)(2,1)S(1)}, bf16[1,64,2048]{2,1,0:T(8,128)(2,1)}, u32[]{:S(2)}) copy-start(bf16[1,64,2048]{2,1,0:T(8,128)(2,1)} %param.5) | copy-start | bytes 786436
  113.7 3.8 %copy-start.4 = (s32[32]{0:T(128)S(1)}, s32[32]{0:T(128)}, u32[]{:S(2)}) copy-start(s32[32]{0:T(128)} %param.9) | copy-start | bytes 388
  113.7 3.9 %copy-start.3 = (s32[32]{0:T(128)S(1)}, s32[32]{0:T(128)}, u32[]{:S(2)}) copy-start(s32[32]{0:T(128)} %param.8) | copy-start | bytes 388
  113.7 4.0 %copy-start.2 = (bf16[32,2048]{1,0:T(8,128)(2,1)S(1)}, bf16[32,2048]{1,0:T(8,128)(2,1)}, u32[]{:S(2)}) copy-start(bf16[32,2048]{1,0:T(8,128)(2,1)} %param.7) | copy-start | bytes 393220
  117.8 6.5 %collective-permute-start = (bf16[32,2048]{1,0:T(8,128)(2,1)S(1)}, bf16[32,2048]{1,0:T(8,128)(2,1)S(1)}, u32[]{:S(2)}, u32[]{:S(2)}) collective-permute-start(bf16[32,2048]{1,0:T(8,128)(2,1)S(1)} %add_select_fusion), channel_id=1, source_target_pairs={{0,16},{1,17},{2,18},{3,19},{4,20},{5,21},{6,22},{7,23},{8,24},{9,... | collective-permute-start | bytes 393224 | tf_op jit(solution)/shard_map/ppermute | solution.py:10
  166.6 3.4 %copy-start = (bf16[1024,2048]{1,0:T(8,128)(2,1)S(1)}, bf16[1024,2048]{1,0:T(8,128)(2,1)}, u32[]{:S(2)}) copy-start(bf16[1024,2048]{1,0:T(8,128)(2,1)} %all-gather.6.cloned.1.call-done) | copy-start | bytes 12582916
  172.1 7.5 %collective-permute-start.1 = (bf16[32,2048]{1,0:T(8,128)(2,1)S(1)}, bf16[32,2048]{1,0:T(8,128)(2,1)S(1)}, u32[]{:S(2)}, u32[]{:S(2)}) collective-permute-start(bf16[32,2048]{1,0:T(8,128)(2,1)S(1)} %pad_maximum_fusion), channel_id=1, source_target_pairs={{16,0},{17,1},{18,2},{19,3},{20,4},{21,5},{22,6},{23,7},{24,8},{25... | collective-permute-start | bytes 393224 | tf_op jit(solution)/shard_map/ppermute | solution.py:10
Sparse Core Ops, SparseCore 0:
  9.5 53.0 all-gather.7
  64.8 48.8 all-gather.9
  117.7 48.8 all-gather.5
where the time goes:
time: 187 us
  waiting for transfers between devices  154 us (82%)
  between operations  13.3 us (7%)
  matrix products  10.4 us (6%)
  starting transfers between devices  4.75 us (3%)
  local copies, waits for them, and re-layouts  2.53 us (1%)
  other arithmetic  1.89 us (1%)
    all_gather x1, waiting for transfers between devices, body(): refl_second = lax.all_gather(refl_local[1], 'blk', axis=0, tiled=True)  53.5 us
    all_gather x1, waiting for transfers between devices, body(): piece_rows = lax.all_gather(trans_local, 'blk', axis=0, tiled=True)  48.1 us
    all_gather x1, waiting for transfers between devices, body(): slab_matrix = lax.all_gather(joined, 'blk', axis=0, tiled=True)  42.3 us
    dot_general x4, matrix products, complex_rows(): product = jnp.dot(stacked, right_matrix, preferred_element_type=jnp.float32)  10.4 us
    ppermute x2, waiting for transfers between devices, shifted(): return lax.ppermute(block, axis, route)  9.38 us
    ppermute x2, starting transfers between devices, shifted(): return lax.ppermute(block, axis, route)  4.67 us
  transfers between devices with their start and end apart: 5, of which 5 were waited for; matrix products, arithmetic and copies ran while one was open for 2% of the time, Pallas kernels for 0%

commit v1 on v0

--- a/solution.py
+++ b/solution.py
@@ -33,7 +33,13 @@
     refl_second = lax.all_gather(refl_local[1], "blk", axis=0, tiled=True)
     coupling = complex_rows(refl_local[0], refl_second).astype(jnp.bfloat16)
     start_rows = trans_local.astype(jnp.float32)
-    piece_rows = lax.all_gather(trans_local, "blk", axis=0, tiled=True)
+    size = lax.axis_size("blk")
+    moving, blocks = (trans_local, [trans_local])
+    for _ in range(size - 1):
+        moving = lax.ppermute(moving, "blk", [(i_2, (i_2 + 1) % size) for i_2 in range(size)])
+        blocks.insert(0, moving)
+    row_of_blocks = jnp.concatenate(blocks, axis=0)
+    piece_rows = jnp.roll(row_of_blocks, (lax.axis_index("blk") + 1) * trans_local.shape[0], axis=0)
     piece_count = piece_rows.shape[0]
     real_cols = lax.slice_in_dim(coupling, 0, piece_count, axis=1)
     imag_cols = lax.dynamic_slice_in_dim(coupling, half_width, piece_count, 1)

time: 187 us -> 258 us (1.38)
  waiting for transfers between devices: 154 us -> 194 us
  local copies, waits for them, and re-layouts: 2.53 us -> 32.9 us
    ppermute x0 -> x15, waiting for transfers between devices: none -> 125 us  [body(): lax.ppermute(moving, 'blk', [(i_2, (i_2 + 1) % size) for i_2 in range(siz...]
    all_gather x1 -> x0, waiting for transfers between devices: 48.1 us -> none  [body(): piece_rows = lax.all_gather(trans_local, 'blk', axis=0, tiled=True)]
    all_gather x1, waiting for transfers between devices: 53.5 us -> 17.2 us  [body(): refl_second = lax.all_gather(refl_local[1], 'blk', axis=0, tiled=True)]
    unnamed x10 -> x45, local copies, waits for them, and re-layouts: 0.19 us -> 28.1 us
  transfers between devices with their start and end apart: 5 -> 19, of which waited for: 5 -> 19; matrix products, arithmetic and copies ran while one was open for 2% -> 12% of each run, Pallas kernels for 0% -> 0%
where the time goes in v1:
time: 258 us
  waiting for transfers between devices  194 us (75%)
  local copies, waits for them, and re-layouts  32.9 us (13%)
  between operations  13.6 us (5%)
  matrix products  10.5 us (4%)
  starting transfers between devices  5.24 us (2%)
    ppermute x15, waiting for transfers between devices, body(): lax.ppermute(moving, 'blk', [(i_2, (i_2 + 1) % size) for i_2 in range(siz...  125 us
    all_gather x1, waiting for transfers between devices, body(): slab_matrix = lax.all_gather(joined, 'blk', axis=0, tiled=True)  42.3 us
    unnamed x45, local copies, waits for them, and re-layouts  28.1 us
    all_gather x1, waiting for transfers between devices, body(): refl_second = lax.all_gather(refl_local[1], 'blk', axis=0, tiled=True)  17.2 us
    dot_general x4, matrix products, complex_rows(): product = jnp.dot(stacked, right_matrix, preferred_element_type=jnp.float32)  10.5 us
    ppermute x2, waiting for transfers between devices, shifted(): return lax.ppermute(block, axis, route)  9.37 us
  transfers between devices with their start and end apart: 19, of which 19 were waited for; matrix products, arithmetic and copies ran while one was open for 12% of the time, Pallas kernels for 0%

profile of v1, /device:TPU:0, one launch (start us, length us, event | category | flops | bytes accessed | tf_op | source)
XLA Modules:
  0.0 258.0 jit_solution(14535312208968174957)
XLA Ops:
  6.5 0.5 collective-permute-start.1
  7.0 9.3 %collective-permute-done.1 = bf16[64,2048]{1,0:T(8,128)(2,1)S(1)} collective-permute-done((bf16[64,2048]{1,0:T(8,128)(2,1)}, bf16[64,2048]{1,0:T(8,128)(2,1)S(1)}, u32[]{:S(2)}, u32[]{:S(2)}) %collective-permute-start.1) | collective-permute-done | bytes 262176 | tf_op jit(solution)/shard_map/ppermute | solution.py:39
  16.3 8.5 %collective-permute-done.2 = bf16[64,2048]{1,0:T(8,128)(2,1)S(1)} collective-permute-done((bf16[64,2048]{1,0:T(8,128)(2,1)S(1)}, bf16[64,2048]{1,0:T(8,128)(2,1)S(1)}, u32[]{:S(2)}, u32[]{:S(2)}) %collective-permute-start.2) | collective-permute-done | bytes 262176 | tf_op jit(solution)/shard_map/ppermute | solution.py:39
  24.8 8.5 %collective-permute-done.3 = bf16[64,2048]{1,0:T(8,128)(2,1)S(1)} collective-permute-done((bf16[64,2048]{1,0:T(8,128)(2,1)S(1)}, bf16[64,2048]{1,0:T(8,128)(2,1)S(1)}, u32[]{:S(2)}, u32[]{:S(2)}) %collective-permute-start.3) | collective-permute-done | bytes 262176 | tf_op jit(solution)/shard_map/ppermute | solution.py:39
  33.3 8.5 %collective-permute-done.4 = bf16[64,2048]{1,0:T(8,128)(2,1)S(1)} collective-permute-done((bf16[64,2048]{1,0:T(8,128)(2,1)S(1)}, bf16[64,2048]{1,0:T(8,128)(2,1)S(1)}, u32[]{:S(2)}, u32[]{:S(2)}) %collective-permute-start.4) | collective-permute-done | bytes 262176 | tf_op jit(solution)/shard_map/ppermute | solution.py:39
  41.8 8.5 %collective-permute-done.5 = bf16[64,2048]{1,0:T(8,128)(2,1)S(1)} collective-permute-done((bf16[64,2048]{1,0:T(8,128)(2,1)S(1)}, bf16[64,2048]{1,0:T(8,128)(2,1)S(1)}, u32[]{:S(2)}, u32[]{:S(2)}) %collective-permute-start.5) | collective-permute-done | bytes 262176 | tf_op jit(solution)/shard_map/ppermute | solution.py:39
  50.3 8.5 %collective-permute-done.6 = bf16[64,2048]{1,0:T(8,128)(2,1)S(1)} collective-permute-done((bf16[64,2048]{1,0:T(8,128)(2,1)S(1)}, bf16[64,2048]{1,0:T(8,128)(2,1)S(1)}, u32[]{:S(2)}, u32[]{:S(2)}) %collective-permute-start.6) | collective-permute-done | bytes 262176 | tf_op jit(solution)/shard_map/ppermute | solution.py:39
  58.8 8.5 %collective-permute-done.7 = bf16[64,2048]{1,0:T(8,128)(2,1)S(1)} collective-permute-done((bf16[64,2048]{1,0:T(8,128)(2,1)S(1)}, bf16[64,2048]{1,0:T(8,128)(2,1)S(1)}, u32[]{:S(2)}, u32[]{:S(2)}) %collective-permute-start.7) | collective-permute-done | bytes 262176 | tf_op jit(solution)/shard_map/ppermute | solution.py:39
  67.3 8.5 %collective-permute-done.8 = bf16[64,2048]{1,0:T(8,128)(2,1)S(1)} collective-permute-done((bf16[64,2048]{1,0:T(8,128)(2,1)S(1)}, bf16[64,2048]{1,0:T(8,128)(2,1)S(1)}, u32[]{:S(2)}, u32[]{:S(2)}) %collective-permute-start.8) | collective-permute-done | bytes 262176 | tf_op jit(solution)/shard_map/ppermute | solution.py:39
  75.8 8.5 %collective-permute-done.9 = bf16[64,2048]{1,0:T(8,128)(2,1)S(1)} collective-permute-done((bf16[64,2048]{1,0:T(8,128)(2,1)S(1)}, bf16[64,2048]{1,0:T(8,128)(2,1)S(1)}, u32[]{:S(2)}, u32[]{:S(2)}) %collective-permute-start.9) | collective-permute-done | bytes 262176 | tf_op jit(solution)/shard_map/ppermute | solution.py:39
  84.3 8.5 %collective-permute-done.10 = bf16[64,2048]{1,0:T(8,128)(2,1)S(1)} collective-permute-done((bf16[64,2048]{1,0:T(8,128)(2,1)S(1)}, bf16[64,2048]{1,0:T(8,128)(2,1)S(1)}, u32[]{:S(2)}, u32[]{:S(2)}) %collective-permute-start.10) | collective-permute-done | bytes 262176 | tf_op jit(solution)/shard_map/ppermute | solution.py:39
  92.8 8.5 %collective-permute-done.11 = bf16[64,2048]{1,0:T(8,128)(2,1)S(1)} collective-permute-done((bf16[64,2048]{1,0:T(8,128)(2,1)S(1)}, bf16[64,2048]{1,0:T(8,128)(2,1)S(1)}, u32[]{:S(2)}, u32[]{:S(2)}) %collective-permute-start.11) | collective-permute-done | bytes 262176 | tf_op jit(solution)/shard_map/ppermute | solution.py:39
  101.3 8.5 %collective-permute-done.12 = bf16[64,2048]{1,0:T(8,128)(2,1)S(1)} collective-permute-done((bf16[64,2048]{1,0:T(8,128)(2,1)S(1)}, bf16[64,2048]{1,0:T(8,128)(2,1)S(1)}, u32[]{:S(2)}, u32[]{:S(2)}) %collective-permute-start.12) | collective-permute-done | bytes 262176 | tf_op jit(solution)/shard_map/ppermute | solution.py:39
  109.8 8.5 %collective-permute-done.13 = bf16[64,2048]{1,0:T(8,128)(2,1)S(1)} collective-permute-done((bf16[64,2048]{1,0:T(8,128)(2,1)S(1)}, bf16[64,2048]{1,0:T(8,128)(2,1)S(1)}, u32[]{:S(2)}, u32[]{:S(2)}) %collective-permute-start.13) | collective-permute-done | bytes 262176 | tf_op jit(solution)/shard_map/ppermute | solution.py:39
  118.3 0.7 copy-done.2
  119.0 8.6 %collective-permute-done.14 = bf16[64,2048]{1,0:T(8,128)(2,1)} collective-permute-done((bf16[64,2048]{1,0:T(8,128)(2,1)S(1)}, bf16[64,2048]{1,0:T(8,128)(2,1)}, u32[]{:S(2)}, u32[]{:S(2)}) %collective-permute-start.14) | collective-permute-done | bytes 262176 | tf_op jit(solution)/shard_map/ppermute | solution.py:39
  127.6 1.9 slice_bitcast_fusion.2
  129.6 1.6 fusion.38
  131.2 5.2 %collective-permute-done.15 = bf16[64,2048]{1,0:T(8,128)(2,1)} collective-permute-done((bf16[64,2048]{1,0:T(8,128)(2,1)}, bf16[64,2048]{1,0:T(8,128)(2,1)}, u32[]{:S(2)}, u32[]{:S(2)}) %collective-permute-start.15) | collective-permute-done | bytes 262176 | tf_op jit(solution)/shard_map/ppermute | solution.py:39
  136.4 1.7 constant_dynamic-update-slice_fusion.31
  138.1 1.7 constant_dynamic-update-slice_fusion.30
  139.7 1.7 constant_dynamic-update-slice_fusion.29
  141.4 0.7 constant_dynamic-update-slice_fusion.28
  142.1 0.7 constant_dynamic-update-slice_fusion.27
  142.8 0.7 constant_dynamic-update-slice_fusion.26
  143.6 0.7 constant_dynamic-update-slice_fusion.25
  144.3 0.7 constant_dynamic-update-slice_fusion.24
  145.0 0.7 constant_dynamic-update-slice_fusion.23
  145.7 0.7 constant_dynamic-update-slice_fusion.22
  146.5 0.7 constant_dynamic-update-slice_fusion.21
  147.2 0.7 constant_dynamic-update-slice_fusion.20
  147.9 0.7 constant_dynamic-update-slice_fusion.19
  148.6 0.7 constant_dynamic-update-slice_fusion.18
  149.3 0.7 constant_dynamic-update-slice_fusion.17
  150.0 0.7 constant_dynamic-update-slice_fusion.16
  150.8 1.7 constant_dynamic-update-slice_fusion.15
  152.5 1.7 constant_dynamic-update-slice_fusion.14
  154.2 0.7 constant_dynamic-update-slice_fusion.13
  154.9 0.7 constant_dynamic-update-slice_fusion.12
  155.6 0.7 constant_dynamic-update-slice_fusion.11
  156.3 0.7 constant_dynamic-update-slice_fusion.10
  157.1 0.7 constant_dynamic-update-slice_fusion.9
  157.8 0.7 constant_dynamic-update-slice_fusion.8
  158.5 0.7 constant_dynamic-update-slice_fusion.7
  159.2 0.7 constant_dynamic-update-slice_fusion.6
  160.0 0.7 constant_dynamic-update-slice_fusion.5
  160.7 0.7 constant_dynamic-update-slice_fusion.4
  161.4 0.7 constant_dynamic-update-slice_fusion.3
  162.1 0.8 constant_dynamic-update-slice_fusion.2
  162.9 0.7 constant_dynamic-update-slice_fusion.1
  163.6 0.7 constant_dynamic-update-slice_fusion
  164.3 17.2 %all-gather.6.cloned.1.call-done = bf16[1,1,1024,2048]{3,2,1,0:T(8,128)(2,1)} async-done(((bf16[1,1,64,2048]{3,2,1,0:T(8,128)(2,1)}), bf16[1,1,1024,2048]{3,2,1,0:T(8,128)(2,1)}) %all-gather.6.cloned.1.call-update) | async-done | bytes 4194320 | tf_op jit(solution)/shard_map/all_gather | solution.py:33
  181.6 3.0 %fusion.4 = f32[128,2048]{1,0:T(8,128)S(1)} fusion(bf16[1,1,1024,2048]{3,2,1,0:T(8,128)(2,1)} %all-gather.6.cloned.1.call-done, bf16[64,1024]{1,0:T(8,128)(2,1)} %get-tuple-element.18, bf16[64,1024]{1,0:T(8,128)(2,1)S(1)} %get-tuple-element.17), kind=kOutput, calls=%fused_computation.4 | convolution fusion | flops 537395200 | bytes 5505024 | tf_op jit(solution)/shard_map/dot_general | solution.py:23
  184.6 2.9 %fusion.6 = f32[128,2048]{1,0:T(8,128)S(1)} fusion(bf16[2048,2048]{1,0:T(8,128)(2,1)} %constant_dynamic-update-slice_fusion, s32[]{:T(128)S(6)} %select_n.26, bf16[64,1024]{1,0:T(8,128)(2,1)S(1)} %get-tuple-element.10, bf16[64,1024]{1,0:T(8,128)(2,1)S(1)} %get-tuple-element.9), kind=kOutput, calls=%fused_computation.6 | convolution fusion | flops 537395200 | bytes 5505028 | tf_op jit(solution)/shard_map/dot_general | solution.py:23
  187.6 0.8 fusion.8
  188.6 3.4 %collective-permute-start = (bf16[32,2048]{1,0:T(8,128)(2,1)S(1)}, bf16[32,2048]{1,0:T(8,128)(2,1)S(1)}, u32[]{:S(2)}, u32[]{:S(2)}) collective-permute-start(bf16[32,2048]{1,0:T(8,128)(2,1)S(1)} %add_select_fusion), channel_id=1, source_target_pairs={{0,16},{1,17},{2,18},{3,19},{4,20},{5,21},{6,22},{7,23},{8,24},{9,... | collective-permute-start | bytes 393224 | tf_op jit(solution)/shard_map/ppermute | solution.py:10
  192.0 3.1 %collective-permute-done = bf16[32,2048]{1,0:T(8,128)(2,1)S(1)} collective-permute-done((bf16[32,2048]{1,0:T(8,128)(2,1)S(1)}, bf16[32,2048]{1,0:T(8,128)(2,1)S(1)}, u32[]{:S(2)}, u32[]{:S(2)}) %collective-permute-start) | collective-permute-done | bytes 131104 | tf_op jit(solution)/shard_map/ppermute | solution.py:10
  195.2 42.3 %all-gather.4.cloned.1.call-done = bf16[1024,2048]{1,0:T(8,128)(2,1)} async-done(((bf16[64,2048]{1,0:T(8,128)(2,1)}), bf16[1024,2048]{1,0:T(8,128)(2,1)}) %all-gather.4.cloned.1.call-update) | async-done | bytes 4194320 | tf_op jit(solution)/shard_map/all_gather | solution.py:48
  237.5 3.2 %fusion.22 = f32[64,2048]{1,0:T(8,128)S(1)} fusion(bf16[1024,2048]{1,0:T(8,128)(2,1)} %all-gather.4.cloned.1.call-done, bf16[32,1024]{1,0:T(8,128)(2,1)S(1)} %get-tuple-element.22, bf16[32,1024]{1,0:T(8,128)(2,1)S(1)} %get-tuple-element.21), kind=kOutput, calls=%fused_computation.40 | convolution fusion | flops 268697600 | bytes 4849664 | tf_op jit(solution)/shard_map/dot_general | solution.py:23
  240.9 0.5 slice_bitcast_fusion.1
  241.5 1.4 fusion
  242.9 1.3 collective-permute-start.16
  244.2 6.2 %collective-permute-done.16 = bf16[32,2048]{1,0:T(8,128)(2,1)S(1)} collective-permute-done((bf16[32,2048]{1,0:T(8,128)(2,1)S(1)}, bf16[32,2048]{1,0:T(8,128)(2,1)S(1)}, u32[]{:S(2)}, u32[]{:S(2)}) %collective-permute-start.16) | collective-permute-done | bytes 131104 | tf_op jit(solution)/shard_map/ppermute | solution.py:10
  250.5 0.7 add_bitcast_fusion
  (42 shorter events, 0.7 us)
Async XLA Ops:
  6.5 143.5 %copy-start.1 = (bf16[1,64,2048]{2,1,0:T(8,128)(2,1)S(1)}, bf16[1,64,2048]{2,1,0:T(8,128)(2,1)}, u32[]{:S(2)}) copy-start(bf16[1,64,2048]{2,1,0:T(8,128)(2,1)} %param.5) | copy-start | bytes 786436
  6.5 175.1 %all-gather.6.cloned.1.call-start = ((), (), s32[]{:S(2)}) async-start(), calls=%async_computation.1 | async-start | bytes 4456448 | tf_op jit(solution)/shard_map/all_gather | solution.py:33
  6.5 9.8 %collective-permute-start.1 = (bf16[64,2048]{1,0:T(8,128)(2,1)}, bf16[64,2048]{1,0:T(8,128)(2,1)S(1)}, u32[]{:S(2)}, u32[]{:S(2)}) collective-permute-start(bf16[64,2048]{1,0:T(8,128)(2,1)} %bitcast.16), channel_id=1, source_target_pairs={{0,1},{1,2},{2,3},{3,4},{4,5},{5,6},{6,7},{7,8},{8,9},{9,10},{10,1... | collective-permute-start | bytes 786440 | tf_op jit(solution)/shard_map/ppermute | solution.py:39
  16.3 8.5 %collective-permute-start.2 = (bf16[64,2048]{1,0:T(8,128)(2,1)S(1)}, bf16[64,2048]{1,0:T(8,128)(2,1)S(1)}, u32[]{:S(2)}, u32[]{:S(2)}) collective-permute-start(bf16[64,2048]{1,0:T(8,128)(2,1)S(1)} %collective-permute-done.1), channel_id=1, source_target_pairs={{0,1},{1,2},{2,3},{3,4},{4,5},{5,6},{6,7},{7,8},{8,9},{9,10},{10,1... | collective-permute-start | bytes 786440 | tf_op jit(solution)/shard_map/ppermute | solution.py:39
  24.8 8.5 %collective-permute-start.3 = (bf16[64,2048]{1,0:T(8,128)(2,1)S(1)}, bf16[64,2048]{1,0:T(8,128)(2,1)S(1)}, u32[]{:S(2)}, u32[]{:S(2)}) collective-permute-start(bf16[64,2048]{1,0:T(8,128)(2,1)S(1)} %collective-permute-done.2), channel_id=1, source_target_pairs={{0,1},{1,2},{2,3},{3,4},{4,5},{5,6},{6,7},{7,8},{8,9},{9,10},{10,1... | collective-permute-start | bytes 786440 | tf_op jit(solution)/shard_map/ppermute | solution.py:39
  33.3 8.5 %collective-permute-start.4 = (bf16[64,2048]{1,0:T(8,128)(2,1)S(1)}, bf16[64,2048]{1,0:T(8,128)(2,1)S(1)}, u32[]{:S(2)}, u32[]{:S(2)}) collective-permute-start(bf16[64,2048]{1,0:T(8,128)(2,1)S(1)} %collective-permute-done.3), channel_id=1, source_target_pairs={{0,1},{1,2},{2,3},{3,4},{4,5},{5,6},{6,7},{7,8},{8,9},{9,10},{10,1... | collective-permute-start | bytes 786440 | tf_op jit(solution)/shard_map/ppermute | solution.py:39
  41.8 8.5 %collective-permute-start.5 = (bf16[64,2048]{1,0:T(8,128)(2,1)S(1)}, bf16[64,2048]{1,0:T(8,128)(2,1)S(1)}, u32[]{:S(2)}, u32[]{:S(2)}) collective-permute-start(bf16[64,2048]{1,0:T(8,128)(2,1)S(1)} %collective-permute-done.4), channel_id=1, source_target_pairs={{0,1},{1,2},{2,3},{3,4},{4,5},{5,6},{6,7},{7,8},{8,9},{9,10},{10,1... | collective-permute-start | bytes 786440 | tf_op jit(solution)/shard_map/ppermute | solution.py:39
  50.3 8.5 %collective-permute-start.6 = (bf16[64,2048]{1,0:T(8,128)(2,1)S(1)}, bf16[64,2048]{1,0:T(8,128)(2,1)S(1)}, u32[]{:S(2)}, u32[]{:S(2)}) collective-permute-start(bf16[64,2048]{1,0:T(8,128)(2,1)S(1)} %collective-permute-done.5), channel_id=1, source_target_pairs={{0,1},{1,2},{2,3},{3,4},{4,5},{5,6},{6,7},{7,8},{8,9},{9,10},{10,1... | collective-permute-start | bytes 786440 | tf_op jit(solution)/shard_map/ppermute | solution.py:39
  58.8 8.5 %collective-permute-start.7 = (bf16[64,2048]{1,0:T(8,128)(2,1)S(1)}, bf16[64,2048]{1,0:T(8,128)(2,1)S(1)}, u32[]{:S(2)}, u32[]{:S(2)}) collective-permute-start(bf16[64,2048]{1,0:T(8,128)(2,1)S(1)} %collective-permute-done.6), channel_id=1, source_target_pairs={{0,1},{1,2},{2,3},{3,4},{4,5},{5,6},{6,7},{7,8},{8,9},{9,10},{10,1... | collective-permute-start | bytes 786440 | tf_op jit(solution)/shard_map/ppermute | solution.py:39
  67.3 8.5 %collective-permute-start.8 = (bf16[64,2048]{1,0:T(8,128)(2,1)S(1)}, bf16[64,2048]{1,0:T(8,128)(2,1)S(1)}, u32[]{:S(2)}, u32[]{:S(2)}) collective-permute-start(bf16[64,2048]{1,0:T(8,128)(2,1)S(1)} %collective-permute-done.7), channel_id=1, source_target_pairs={{0,1},{1,2},{2,3},{3,4},{4,5},{5,6},{6,7},{7,8},{8,9},{9,10},{10,1... | collective-permute-start | bytes 786440 | tf_op jit(solution)/shard_map/ppermute | solution.py:39
  75.8 8.5 %collective-permute-start.9 = (bf16[64,2048]{1,0:T(8,128)(2,1)S(1)}, bf16[64,2048]{1,0:T(8,128)(2,1)S(1)}, u32[]{:S(2)}, u32[]{:S(2)}) collective-permute-start(bf16[64,2048]{1,0:T(8,128)(2,1)S(1)} %collective-permute-done.8), channel_id=1, source_target_pairs={{0,1},{1,2},{2,3},{3,4},{4,5},{5,6},{6,7},{7,8},{8,9},{9,10},{10,1... | collective-permute-start | bytes 786440 | tf_op jit(solution)/shard_map/ppermute | solution.py:39
  84.3 8.5 %collective-permute-start.10 = (bf16[64,2048]{1,0:T(8,128)(2,1)S(1)}, bf16[64,2048]{1,0:T(8,128)(2,1)S(1)}, u32[]{:S(2)}, u32[]{:S(2)}) collective-permute-start(bf16[64,2048]{1,0:T(8,128)(2,1)S(1)} %collective-permute-done.9), channel_id=1, source_target_pairs={{0,1},{1,2},{2,3},{3,4},{4,5},{5,6},{6,7},{7,8},{8,9},{9,10},{10,1... | collective-permute-start | bytes 786440 | tf_op jit(solution)/shard_map/ppermute | solution.py:39
  92.8 8.5 %collective-permute-start.11 = (bf16[64,2048]{1,0:T(8,128)(2,1)S(1)}, bf16[64,2048]{1,0:T(8,128)(2,1)S(1)}, u32[]{:S(2)}, u32[]{:S(2)}) collective-permute-start(bf16[64,2048]{1,0:T(8,128)(2,1)S(1)} %collective-permute-done.10), channel_id=1, source_target_pairs={{0,1},{1,2},{2,3},{3,4},{4,5},{5,6},{6,7},{7,8},{8,9},{9,10},{10,1... | collective-permute-start | bytes 786440 | tf_op jit(solution)/shard_map/ppermute | solution.py:39
  101.3 8.5 %collective-permute-start.12 = (bf16[64,2048]{1,0:T(8,128)(2,1)S(1)}, bf16[64,2048]{1,0:T(8,128)(2,1)S(1)}, u32[]{:S(2)}, u32[]{:S(2)}) collective-permute-start(bf16[64,2048]{1,0:T(8,128)(2,1)S(1)} %collective-permute-done.11), channel_id=1, source_target_pairs={{0,1},{1,2},{2,3},{3,4},{4,5},{5,6},{6,7},{7,8},{8,9},{9,10},{10,1... | collective-permute-start | bytes 786440 | tf_op jit(solution)/shard_map/ppermute | solution.py:39
  109.8 8.5 %collective-permute-start.13 = (bf16[64,2048]{1,0:T(8,128)(2,1)S(1)}, bf16[64,2048]{1,0:T(8,128)(2,1)S(1)}, u32[]{:S(2)}, u32[]{:S(2)}) collective-permute-start(bf16[64,2048]{1,0:T(8,128)(2,1)S(1)} %collective-permute-done.12), channel_id=1, source_target_pairs={{0,1},{1,2},{2,3},{3,4},{4,5},{5,6},{6,7},{7,8},{8,9},{9,10},{10,1... | collective-permute-start | bytes 786440 | tf_op jit(solution)/shard_map/ppermute | solution.py:39
  118.3 0.7 copy-start.2
  119.0 8.6 %collective-permute-start.14 = (bf16[64,2048]{1,0:T(8,128)(2,1)S(1)}, bf16[64,2048]{1,0:T(8,128)(2,1)}, u32[]{:S(2)}, u32[]{:S(2)}) collective-permute-start(bf16[64,2048]{1,0:T(8,128)(2,1)S(1)} %collective-permute-done.13), channel_id=1, source_target_pairs={{0,1},{1,2},{2,3},{3,4},{4,5},{5,6},{6,7},{7,8},{8,9},{9,10},{10,1... | collective-permute-start | bytes 786440 | tf_op jit(solution)/shard_map/ppermute | solution.py:39
  127.6 8.8 %collective-permute-start.15 = (bf16[64,2048]{1,0:T(8,128)(2,1)}, bf16[64,2048]{1,0:T(8,128)(2,1)}, u32[]{:S(2)}, u32[]{:S(2)}) collective-permute-start(bf16[64,2048]{1,0:T(8,128)(2,1)} %collective-permute-done.14), channel_id=1, source_target_pairs={{0,1},{1,2},{2,3},{3,4},{4,5},{5,6},{6,7},{7,8},{8,9},{9,10},{10,1... | collective-permute-start | bytes 786440 | tf_op jit(solution)/shard_map/ppermute | solution.py:39
  129.5 108.0 %all-gather.4.cloned.1.call-start = ((), (), s32[]{:S(2)}) async-start(), calls=%async_computation | async-start | bytes 4456448 | tf_op jit(solution)/shard_map/all_gather | solution.py:48
  131.2 23.0 %copy-start.3 = (bf16[64,2048]{1,0:T(8,128)(2,1)S(1)}, bf16[64,2048]{1,0:T(8,128)(2,1)}, u32[]{:S(2)}) copy-start(bf16[64,2048]{1,0:T(8,128)(2,1)} %copy-done.2) | copy-start | bytes 786436
  162.1 26.3 %copy-start.6 = (s32[32]{0:T(128)S(1)}, s32[32]{0:T(128)}, u32[]{:S(2)}) copy-start(s32[32]{0:T(128)} %param.9) | copy-start | bytes 388
  162.1 26.3 %copy-start.5 = (s32[32]{0:T(128)S(1)}, s32[32]{0:T(128)}, u32[]{:S(2)}) copy-start(s32[32]{0:T(128)} %param.8) | copy-start | bytes 388
  162.1 26.5 %copy-start.4 = (bf16[32,2048]{1,0:T(8,128)(2,1)S(1)}, bf16[32,2048]{1,0:T(8,128)(2,1)}, u32[]{:S(2)}) copy-start(bf16[32,2048]{1,0:T(8,128)(2,1)} %param.7) | copy-start | bytes 393220
  188.6 6.5 %collective-permute-start = (bf16[32,2048]{1,0:T(8,128)(2,1)S(1)}, bf16[32,2048]{1,0:T(8,128)(2,1)S(1)}, u32[]{:S(2)}, u32[]{:S(2)}) collective-permute-start(bf16[32,2048]{1,0:T(8,128)(2,1)S(1)} %add_select_fusion), channel_id=1, source_target_pairs={{0,16},{1,17},{2,18},{3,19},{4,20},{5,21},{6,22},{7,23},{8,24},{9,... | collective-permute-start | bytes 393224 | tf_op jit(solution)/shard_map/ppermute | solution.py:10
  237.5 3.4 %copy-start = (bf16[1024,2048]{1,0:T(8,128)(2,1)S(1)}, bf16[1024,2048]{1,0:T(8,128)(2,1)}, u32[]{:S(2)}) copy-start(bf16[1024,2048]{1,0:T(8,128)(2,1)} %all-gather.4.cloned.1.call-done) | copy-start | bytes 12582916
  242.9 7.5 %collective-permute-start.16 = (bf16[32,2048]{1,0:T(8,128)(2,1)S(1)}, bf16[32,2048]{1,0:T(8,128)(2,1)S(1)}, u32[]{:S(2)}, u32[]{:S(2)}) collective-permute-start(bf16[32,2048]{1,0:T(8,128)(2,1)S(1)} %pad_maximum_fusion), channel_id=1, source_target_pairs={{16,0},{17,1},{18,2},{19,3},{20,4},{21,5},{22,6},{23,7},{24,8},{25... | collective-permute-start | bytes 393224 | tf_op jit(solution)/shard_map/ppermute | solution.py:10
Sparse Core Ops, SparseCore 0:
  129.6 51.9 all-gather.5
  188.5 48.9 all-gather.3
